TPU v7x, 512 devices: a whole 4x4x16 slice. The times are simulated.
512 devices in a mesh: branch: 8 (over z_lo), dp: 64 (over x, y, z_hi, core).
Axes of the slice: x: 4, y: 4, z: 16 (z_hi: 2, z_lo: 8; z = z_hi * 8 + z_lo), core: 2. Of those that a mesh axis runs over, the one named last changes fastest.
Arguments:
- tokens: bfloat16 [512, 4096], P('dp'), may hold values from -6 to 6
- routes: int32 [512, 2], P('dp'), may hold values from 0 to 7, all different within a row; in each aligned block of 8 rows (0 to 7, 8 to 15, ...) at most 4 rows name the same one
- route_weights: float32 [512, 2], P('dp'), may hold values from 0.2 to 1
- norm_gains: float32 [8, 4096], P('branch'), may hold values from 0.25 to 1.75
- keyval_weights: bfloat16 [8, 4096, 2048], P('branch', 'dp'), may hold values from -0.09375 to 0.09375
- expert_gate: bfloat16 [8, 4096, 8192], P('branch', None, 'dp'), may hold values from -0.09375 to 0.09375
- expert_up: bfloat16 [8, 4096, 8192], P('branch', None, 'dp'), may hold values from -0.09375 to 0.09375
- expert_down: bfloat16 [8, 8192, 4096], P('branch', None, 'dp'), may hold values from -0.0625 to 0.0625
Outputs:
- mixed: bfloat16 [512, 4096], P('dp')
- merged_keyval: bfloat16 [4096, 2048], P('dp', 'branch')
Inputs may be any that keep to these rules, and one draw needn't show every extreme that they name: `routes`: each token names 2 different experts. Among the 8 tokens of one dp index at most 4 name one expert, a bound that some block reaches.
All inputs are finite; a program needn't handle non-finite values.
Results may differ from a plain program's by a relative error of at most 0.013.
Values may be sent and summed in bfloat16 or wider, within the bound.
No kernel may reach another device: no remote copies, remote signals or barrier semaphores. Data moves between devices by JAX's collectives and lax.ppermute only.
A program may use at most 64 MiB of HBM per device.

v0:
```python
import jax
import jax.numpy as jnp
from jax import lax
from jax.sharding import PartitionSpec as P


def merge_keyval(keyval_weights, branches):
    summed = lax.psum_scatter(
        keyval_weights[0].astype(jnp.float32).astype(jnp.bfloat16),
        "branch",
        scatter_dimension=1,
        tiled=True,
    ).astype(jnp.float32)
    return (summed / branches).astype(jnp.bfloat16)


def normalize(block_rows, gain_avg):
    widened = block_rows.astype(jnp.float32)
    inv_rms = lax.rsqrt(jnp.mean(widened * widened, axis=1, keepdims=True) + 1e-05)
    return (widened * inv_rms * gain_avg[None, :]).astype(jnp.bfloat16)


def local(
    tokens, routes, route_weights, norm_gains, keyval_weights, expert_gate, expert_up, expert_down
):
    branches = lax.axis_size("branch")
    expert = lax.axis_index("branch")
    tok_count = tokens.shape[0]
    capacity = min(tok_count, 4 * tok_count // branches)
    merged_keyval = merge_keyval(keyval_weights, branches)
    gain_avg = lax.psum(norm_gains[0], "branch") / branches
    matched = routes == expert
    chosen = jnp.any(matched, axis=1)
    weight_share = jnp.sum(jnp.where(matched, route_weights, jnp.zeros_like(route_weights)), axis=1)
    slot_index = jnp.cumsum(chosen.astype(jnp.int32)) - 1
    picks = (
        (slot_index[None, :] == jnp.arange(capacity, dtype=jnp.int32)[:, None]) & chosen[None, :]
    ).astype(jnp.bfloat16)
    source_rows = normalize(tokens, gain_avg)
    packed = jnp.dot(picks, source_rows, preferred_element_type=jnp.float32).astype(jnp.bfloat16)
    block_rows = lax.all_gather(packed, "dp", axis=0, tiled=True)
    gate_part = jnp.dot(block_rows, expert_gate[0], preferred_element_type=jnp.float32)
    up_part = jnp.dot(block_rows, expert_up[0], preferred_element_type=jnp.float32)
    hidden = (jax.nn.silu(gate_part) * up_part).astype(jnp.bfloat16)
    down_rows = expert_down[0]
    result_cols = lax.dot_general(
        down_rows,
        lax.all_gather(hidden, "dp", axis=1, tiled=True),
        (((0,), (1,)), ((), ())),
        preferred_element_type=jnp.float32,
    ).astype(jnp.bfloat16)
    own_slots = lax.all_to_all(result_cols, "dp", split_axis=1, concat_axis=0, tiled=True)
    returned = (
        lax.dot_general(
            picks, own_slots, (((0,), (1,)), ((), ())), preferred_element_type=jnp.float32
        )
        * weight_share[:, None]
    )
    expert_total = lax.psum(returned, "branch")
    mixed = (tokens.astype(jnp.float32) + expert_total).astype(jnp.bfloat16)
    return (mixed, merged_keyval)


def solution(mesh):
    in_specs = (
        P("dp", None),
        P("dp", None),
        P("dp", None),
        P("branch", None),
        P("branch", "dp", None),
        P("branch", None, "dp"),
        P("branch", None, "dp"),
        P("branch", None, "dp"),
    )
    out_specs = (P("dp", None), P("dp", "branch"))
    return jax.shard_map(local, mesh=mesh, in_specs=in_specs, out_specs=out_specs, check_vma=False)
```

profile of v0, /device:TPU:2, one launch (start us, length us, event | category | flops | bytes accessed | tf_op | source)
XLA Modules:
  0.0 531.0 jit_solution(3716925837076763852)
XLA Ops:
  8.1 0.8 fusion.21
  8.8 0.2 reduce-window.8
  9.0 59.9 %psum.14 = f32[4096]{0:T(1024)S(1)} all-reduce(f32[4096]{0:T(1024)} %bitcast.33), channel_id=1, replica_groups=mesh['branch'=8,'dp'=64] {'branch'}, use_global_device_ids=true, to_apply=%region_3.4 | all-reduce | flops 4096 | bytes 32768 | tf_op jit(solution)/shard_map/psum | solution.py:31
  68.9 1.0 fusion.7
  69.9 1.7 fusion
  71.7 108.6 %all-gather.6.cloned.1.call-done = bf16[64,4,4096]{2,1,0:T(4,128)(2,1)} async-done(((bf16[1,4,4096]{2,1,0:T(4,128)(2,1)}), bf16[64,4,4096]{2,1,0:T(4,128)(2,1)}) %all-gather.6.cloned.1.call-update) | async-done | bytes 2097168 | tf_op jit(solution)/shard_map/all_gather | solution.py:41
  180.3 2.5 reshape.52
  182.9 0.7 fusion.5
  183.6 0.5 copy-done.4
  184.1 1.3 fusion.1
  185.5 134.4 %all-gather.4.cloned.1.call-done = bf16[256,8192]{1,0:T(8,128)(2,1)} async-done(((bf16[256,128]{1,0:T(8,128)(2,1)}), bf16[256,8192]{1,0:T(8,128)(2,1)}) %all-gather.4.cloned.1.call-update) | async-done | bytes 4194320 | tf_op jit(solution)/shard_map/all_gather | solution.py:48
  319.9 3.9 fusion.2
  323.8 0.1 copy.12
  323.9 0.7 reshape.53
  324.6 7.4 %all-to-all-start = ((bf16[64,2,128]{2,1,0:T(2,128)(2,1)}), bf16[64,2,128]{2,1,0:T(2,128)(2,1)S(1)}, u32[]{:S(2)}, u32[]{:S(2)}) async-start(bf16[64,2,128]{2,1,0:T(2,128)(2,1)} %reshape.53), calls=%async_computation | async-start | bytes 65536 | tf_op jit(solution)/shard_map/all_to_all | solution.py:52
  332.1 0.5 reduce-scatter.2.cloned.1.call-update
  332.7 15.1 %all-to-all-done = bf16[64,2,128]{2,1,0:T(2,128)(2,1)S(1)} async-done(((bf16[64,2,128]{2,1,0:T(2,128)(2,1)}), bf16[64,2,128]{2,1,0:T(2,128)(2,1)S(1)}, u32[]{:S(2)}, u32[]{:S(2)}) %all-to-all-start) | async-done | bytes 32800 | tf_op jit(solution)/shard_map/all_to_all | solution.py:52
  347.8 0.1 reshape.54
  348.0 0.1 all_to_all.17
  348.1 0.9 convolution_multiply_fusion
  349.0 55.0 %reduce-scatter.2.cloned.1.call-done = bf16[64,256]{1,0:T(8,128)(2,1)} async-done(((bf16[64,2048]{1,0:T(8,128)(2,1)}), bf16[64,256]{1,0:T(8,128)(2,1)}) %reduce-scatter.2.cloned.1.call-update) | async-done | bytes 32784 | tf_op jit(solution)/shard_map/reduce_scatter | solution.py:8
  404.0 1.4 multiply_convert_fusion
  405.3 116.7 %all-reduce.2.cloned.1.call-done = f32[8,4096]{1,0:T(8,128)} async-done(((f32[8,4096]{1,0:T(8,128)}), f32[8,4096]{1,0:T(8,128)}) %all-reduce.2.cloned.1.call-update) | async-done | bytes 131088 | tf_op jit(solution)/shard_map/psum | solution.py:59
  522.1 1.5 fusion.10
  (23 shorter events, 0.3 us)
Async XLA Ops:
  8.0 174.8 %copy-start = (bf16[1,4096,128]{2,1,0:T(8,128)(2,1)S(1)}, bf16[1,4096,128]{2,1,0:T(8,128)(2,1)}, u32[]{:S(2)}) copy-start(bf16[1,4096,128]{2,1,0:T(8,128)(2,1)} %param.13) | copy-start | bytes 3145732
  8.0 172.3 %all-gather.6.cloned.1.call-start = ((), (), s32[]{:S(2)}) async-start(), calls=%async_computation.5 | async-start | bytes 2129920 | tf_op jit(solution)/shard_map/all_gather | solution.py:41
  71.6 248.3 %all-gather.4.cloned.1.call-start = ((), (), s32[]{:S(2)}) async-start(), calls=%async_computation.2 | async-start | bytes 4259840 | tf_op jit(solution)/shard_map/all_gather | solution.py:48
  182.8 1.2 copy-start.4
  185.4 147.3 %copy-start.2 = (s32[8,2]{0,1:T(2,128)S(1)}, s32[8,2]{0,1:T(2,128)}, u32[]{:S(2)}) copy-start(s32[8,2]{0,1:T(2,128)} %param.9) | copy-start | bytes 196
  185.4 147.3 %copy-start.3 = (f32[8,2]{0,1:T(2,128)S(1)}, f32[8,2]{0,1:T(2,128)}, u32[]{:S(2)}) copy-start(f32[8,2]{0,1:T(2,128)} %param.10) | copy-start | bytes 196
  185.5 336.6 %copy-start.1 = (bf16[8,4096]{1,0:T(8,128)(2,1)S(1)}, bf16[8,4096]{1,0:T(8,128)(2,1)}, u32[]{:S(2)}) copy-start(bf16[8,4096]{1,0:T(8,128)(2,1)} %param.8) | copy-start | bytes 196612
  324.6 23.2 %all-to-all-start = ((bf16[64,2,128]{2,1,0:T(2,128)(2,1)}), bf16[64,2,128]{2,1,0:T(2,128)(2,1)S(1)}, u32[]{:S(2)}, u32[]{:S(2)}) async-start(bf16[64,2,128]{2,1,0:T(2,128)(2,1)} %reshape.53), calls=%async_computation | async-start | bytes 65536 | tf_op jit(solution)/shard_map/all_to_all | solution.py:52
  332.1 71.9 %reduce-scatter.2.cloned.1.call-start = ((), (), s32[]{:S(2)}) async-start(), calls=%async_computation.4 | async-start | bytes 294912 | tf_op jit(solution)/shard_map/reduce_scatter | solution.py:8
  332.6 189.4 %all-reduce.2.cloned.1.call-start = ((), (), s32[]{:S(2)}) async-start(), calls=%async_computation.3 | async-start | bytes 262144 | tf_op jit(solution)/shard_map/psum | solution.py:59
Sparse Core Ops, SparseCore 0:
  71.7 108.5 all-gather.5
  185.6 134.2 all-gather.3
Sparse Core Ops, SparseCore 1:
  335.3 68.6 reduce-scatter.1
  406.7 115.3 all-reduce.1
where the time goes:
time: 532 us; the launch traced here: 531 us
  waiting for transfers between devices  430 us (81%)
  blocking collectives  59.9 us (11%)
  between operations  15.6 us (3%)
  matrix products  8.44 us (2%)
  starting transfers between devices  7.61 us (1%)
    all_gather x1, waiting for transfers between devices, local(): lax.all_gather(hidden, 'dp', axis=1, tiled=True)  134 us
    psum x1, waiting for transfers between devices, local(): expert_total = lax.psum(returned, 'branch')  117 us
    all_gather x1, waiting for transfers between devices, local(): block_rows = lax.all_gather(packed, 'dp', axis=0, tiled=True)  109 us
    psum x1, blocking collectives, local(): gain_avg = lax.psum(norm_gains[0], 'branch') / branches  59.9 us
    reduce_scatter x1, waiting for transfers between devices, merge_keyval(): lax.psum_scatter(keyval_weights[0].astype(jnp.float32).astype(jnp.bfloat1...  55 us
    all_to_all x1, waiting for transfers between devices, local(): lax.all_to_all(result_cols, 'dp', split_axis=1, concat_axis=0, tiled=True)  15.1 us
  transfers between devices with their start and end apart: 5, of which 5 were waited for; matrix products, arithmetic and copies ran while one was open for 0% of the time, Pallas kernels for 0%

commit v1 on v0

--- a/solution.py
+++ b/solution.py
@@ -56,7 +56,7 @@
         )
         * weight_share[:, None]
     )
-    expert_total = lax.psum(returned, "branch")
+    expert_total = jnp.sum(lax.all_gather(returned, "branch"), axis=0)
     mixed = (tokens.astype(jnp.float32) + expert_total).astype(jnp.bfloat16)
     return (mixed, merged_keyval)
 

time: 532 us -> 477 us (0.90)
  waiting for transfers between devices: 430 us -> 376 us
    psum x1 -> x0, waiting for transfers between devices: 117 us -> none  [local(): expert_total = lax.psum(returned, 'branch')]
    all_gather x0 -> x1, waiting for transfers between devices: none -> 61.9 us  [local(): expert_total = jnp.sum(lax.all_gather(returned, 'branch'), axis=0)]
  transfers between devices with their start and end apart: 5 -> 5, of which waited for: 5 -> 5; matrix products, arithmetic and copies ran while one was open for 0% -> 1% of each run, Pallas kernels for 0% -> 0%
where the time goes in v1:
time: 477 us
  waiting for transfers between devices  376 us (79%)
  blocking collectives  59.9 us (13%)
  between operations  15.6 us (3%)
  matrix products  8.44 us (2%)
  starting transfers between devices  7.61 us (2%)
  other arithmetic  5.31 us (1%)
    all_gather x1, waiting for transfers between devices, local(): lax.all_gather(hidden, 'dp', axis=1, tiled=True)  134 us
    all_gather x1, waiting for transfers between devices, local(): block_rows = lax.all_gather(packed, 'dp', axis=0, tiled=True)  109 us
    all_gather x1, waiting for transfers between devices, local(): expert_total = jnp.sum(lax.all_gather(returned, 'branch'), axis=0)  61.9 us
    psum x1, blocking collectives, local(): gain_avg = lax.psum(norm_gains[0], 'branch') / branches  59.9 us
    reduce_scatter x1, waiting for transfers between devices, merge_keyval(): lax.psum_scatter(keyval_weights[0].astype(jnp.float32).astype(jnp.bfloat1...  55 us
    all_to_all x1, waiting for transfers between devices, local(): lax.all_to_all(result_cols, 'dp', split_axis=1, concat_axis=0, tiled=True)  15.1 us
  transfers between devices with their start and end apart: 5, of which 5 were waited for; matrix products, arithmetic and copies ran while one was open for 1% of the time, Pallas kernels for 0%

profile of v1, /device:TPU:2, one launch (start us, length us, event | category | flops | bytes accessed | tf_op | source)
XLA Modules:
  0.0 476.6 jit_solution(3314857556598803051)
XLA Ops:
  8.1 0.8 fusion.21
  8.8 0.2 reduce-window.8
  9.0 59.9 %psum.7 = f32[4096]{0:T(1024)S(1)} all-reduce(f32[4096]{0:T(1024)} %bitcast.35), channel_id=1, replica_groups=mesh['branch'=8,'dp'=64] {'branch'}, use_global_device_ids=true, to_apply=%region_3.4 | all-reduce | flops 4096 | bytes 32768 | tf_op jit(solution)/shard_map/psum | solution.py:31
  68.9 1.0 fusion.7
  69.9 1.7 fusion
  71.7 108.6 %all-gather.10.cloned.1.call-done = bf16[64,4,4096]{2,1,0:T(4,128)(2,1)} async-done(((bf16[1,4,4096]{2,1,0:T(4,128)(2,1)}), bf16[64,4,4096]{2,1,0:T(4,128)(2,1)}) %all-gather.10.cloned.1.call-update) | async-done | bytes 2097168 | tf_op jit(solution)/shard_map/all_gather | solution.py:41
  180.3 2.5 reshape.53
  182.9 0.7 fusion.5
  183.6 0.5 copy-done.4
  184.1 1.3 fusion.1
  185.5 134.4 %all-gather.6.cloned.1.call-done = bf16[256,8192]{1,0:T(8,128)(2,1)} async-done(((bf16[256,128]{1,0:T(8,128)(2,1)}), bf16[256,8192]{1,0:T(8,128)(2,1)}) %all-gather.6.cloned.1.call-update) | async-done | bytes 4194320 | tf_op jit(solution)/shard_map/all_gather | solution.py:48
  319.9 3.9 fusion.2
  323.8 0.1 copy.12
  323.9 0.7 reshape.54
  324.6 7.4 %all-to-all-start = ((bf16[64,2,128]{2,1,0:T(2,128)(2,1)}), bf16[64,2,128]{2,1,0:T(2,128)(2,1)S(1)}, u32[]{:S(2)}, u32[]{:S(2)}) async-start(bf16[64,2,128]{2,1,0:T(2,128)(2,1)} %reshape.54), calls=%async_computation | async-start | bytes 65536 | tf_op jit(solution)/shard_map/all_to_all | solution.py:52
  332.1 0.5 reduce-scatter.2.cloned.1.call-update
  332.7 15.1 %all-to-all-done = bf16[64,2,128]{2,1,0:T(2,128)(2,1)S(1)} async-done(((bf16[64,2,128]{2,1,0:T(2,128)(2,1)}), bf16[64,2,128]{2,1,0:T(2,128)(2,1)S(1)}, u32[]{:S(2)}, u32[]{:S(2)}) %all-to-all-start) | async-done | bytes 32800 | tf_op jit(solution)/shard_map/all_to_all | solution.py:52
  348.0 0.1 all_to_all.17
  348.1 0.9 convolution_multiply_fusion
  349.0 55.0 %reduce-scatter.2.cloned.1.call-done = bf16[64,256]{1,0:T(8,128)(2,1)} async-done(((bf16[64,2048]{1,0:T(8,128)(2,1)}), bf16[64,256]{1,0:T(8,128)(2,1)}) %reduce-scatter.2.cloned.1.call-update) | async-done | bytes 32784 | tf_op jit(solution)/shard_map/reduce_scatter | solution.py:8
  404.0 1.4 multiply_convert_fusion
  405.3 61.9 %all-gather.8.cloned.1.call-done = f32[64,4096]{1,0:T(8,128)} async-done(((f32[8,4096]{1,0:T(8,128)}), f32[64,4096]{1,0:T(8,128)}) %all-gather.8.cloned.1.call-update) | async-done | bytes 1048592 | tf_op jit(solution)/shard_map/all_gather | solution.py:59
  467.3 1.3 bitcast_reduce_fusion
  468.6 0.6 fusion.10
  (24 shorter events, 0.4 us)
Async XLA Ops:
  8.0 174.8 %copy-start = (bf16[1,4096,128]{2,1,0:T(8,128)(2,1)S(1)}, bf16[1,4096,128]{2,1,0:T(8,128)(2,1)}, u32[]{:S(2)}) copy-start(bf16[1,4096,128]{2,1,0:T(8,128)(2,1)} %param.13) | copy-start | bytes 3145732
  8.0 172.3 %all-gather.10.cloned.1.call-start = ((), (), s32[]{:S(2)}) async-start(), calls=%async_computation.5 | async-start | bytes 2129920 | tf_op jit(solution)/shard_map/all_gather | solution.py:41
  71.6 248.3 %all-gather.6.cloned.1.call-start = ((), (), s32[]{:S(2)}) async-start(), calls=%async_computation.2 | async-start | bytes 4259840 | tf_op jit(solution)/shard_map/all_gather | solution.py:48
  182.8 1.2 copy-start.4
  185.4 147.3 %copy-start.2 = (s32[8,2]{0,1:T(2,128)S(1)}, s32[8,2]{0,1:T(2,128)}, u32[]{:S(2)}) copy-start(s32[8,2]{0,1:T(2,128)} %param.9) | copy-start | bytes 196
  185.4 147.3 %copy-start.3 = (f32[8,2]{0,1:T(2,128)S(1)}, f32[8,2]{0,1:T(2,128)}, u32[]{:S(2)}) copy-start(f32[8,2]{0,1:T(2,128)} %param.10) | copy-start | bytes 196
  323.8 144.8 %copy-start.1 = (bf16[8,4096]{1,0:T(8,128)(2,1)S(1)}, bf16[8,4096]{1,0:T(8,128)(2,1)}, u32[]{:S(2)}) copy-start(bf16[8,4096]{1,0:T(8,128)(2,1)} %param.8) | copy-start | bytes 196612
  324.6 23.2 %all-to-all-start = ((bf16[64,2,128]{2,1,0:T(2,128)(2,1)}), bf16[64,2,128]{2,1,0:T(2,128)(2,1)S(1)}, u32[]{:S(2)}, u32[]{:S(2)}) async-start(bf16[64,2,128]{2,1,0:T(2,128)(2,1)} %reshape.54), calls=%async_computation | async-start | bytes 65536 | tf_op jit(solution)/shard_map/all_to_all | solution.py:52
  332.1 71.9 %reduce-scatter.2.cloned.1.call-start = ((), (), s32[]{:S(2)}) async-start(), calls=%async_computation.3 | async-start | bytes 294912 | tf_op jit(solution)/shard_map/reduce_scatter | solution.py:8
  332.6 134.6 %all-gather.8.cloned.1.call-start = ((), (), s32[]{:S(2)}) async-start(), calls=%async_computation.4 | async-start | bytes 1179648 | tf_op jit(solution)/shard_map/all_gather | solution.py:59
Sparse Core Ops, SparseCore 0:
  71.7 108.5 all-gather.9
  185.6 134.2 all-gather.5
Sparse Core Ops, SparseCore 1:
  335.3 68.6 reduce-scatter.1
  405.9 61.3 all-gather.7
